TPU v7x, 256 devices: a whole 4x4x8 slice. The times are simulated.
256 devices in a mesh: row: 8 (over x, core), col: 32 (over z, y).
Axes of the slice: x: 4, y: 4, z: 8, core: 2. Of those that a mesh axis runs over, the one named last changes fastest.
Arguments:
- source_pcs: bfloat16 [32768, 64], P('row'), may hold values from -8 to 8
- target_pcs: bfloat16 [131072, 64], P('col'), may hold values from -8 to 8
- source_mass: float32 [32768], P('row'), may hold values from 0.25 to 4
- target_mass: float32 [131072], P('col'), may hold values from 0.25 to 4
- source_scaling: float32 [32768], P('row'), may hold values from 0.1 to 10
- labels: int32 [131072], P('col'), may hold values from 0 to 31
Outputs:
- fates: float32 [32768, 32], P(('row', 'col'))
- source_potential: float32 [32768], P(('row', 'col'))
- target_potential: float32 [131072], P('col')
All inputs are finite; a program needn't handle non-finite values.
Results may differ from a plain program's by a relative error of at most 0.00035.
Values may be sent and summed in bfloat16 or wider, within the bound.
No kernel may reach another device: no remote copies, remote signals or barrier semaphores. Data moves between devices by JAX's collectives and lax.ppermute only.
A program may use at most 128 MiB of HBM per device.

v0:
```python
import jax
import jax.numpy as jnp
from jax import lax
from jax.sharding import PartitionSpec as P

SETS = 32
ITERS = 2
entropy_weight = 0.5
offset_small = 1e-06


def kernel_rows(source_pcs, source_sq, target_pcs, target_sq, inverse, first_row, row_count):
    source_block = lax.dynamic_slice_in_dim(source_pcs, first_row, row_count, 0)
    block_sq = lax.dynamic_slice_in_dim(source_sq, first_row, row_count, 0)
    inner_products = lax.dot_general(
        source_block, target_pcs, (((1,), (1,)), ((), ())), preferred_element_type=jnp.float32
    )
    exponent = (block_sq[:, None] + target_sq[None, :] - 2.0 * inner_products) * inverse
    return jnp.exp(-exponent).astype(jnp.bfloat16)


def on_device(source_pcs, target_pcs, source_mass, target_mass, source_scaling, labels):
    row_count = source_pcs.shape[0]
    col_count = target_pcs.shape[0]
    source_wide = source_pcs.astype(jnp.float32)
    target_wide = target_pcs.astype(jnp.float32)
    source_sq = jnp.sum(source_wide * source_wide, 1)
    target_sq = jnp.sum(target_wide * target_wide, 1)
    source_sum, source_sqsum = lax.psum((jnp.sum(source_wide, 0), jnp.sum(source_sq)), "row")
    target_sum, target_sqsum = lax.psum((jnp.sum(target_wide, 0), jnp.sum(target_sq)), "col")
    source_total = row_count * lax.axis_size("row")
    target_total = col_count * lax.axis_size("col")
    mean_square = (
        source_sqsum / source_total
        + target_sqsum / target_total
        - 2.0 * jnp.sum(source_sum / source_total * (target_sum / target_total))
        + offset_small
    )
    inverse = 1.0 / (entropy_weight * mean_square)
    block_rows = min(row_count, 512)
    block_count = row_count // block_rows

    def one_block(block_index):
        return kernel_rows(
            source_pcs,
            source_sq,
            target_pcs,
            target_sq,
            inverse,
            block_index * block_rows,
            block_rows,
        )

    kernel = lax.map(one_block, jnp.arange(block_count, dtype=jnp.int32)).reshape(
        row_count, col_count
    )

    def row_pass(right_side):
        return jnp.dot(kernel, right_side, preferred_element_type=jnp.float32)

    share_rows = row_count // lax.axis_size("col")
    own_first = lax.axis_index("col") * share_rows
    own_mass = lax.dynamic_slice_in_dim(source_mass, own_first, share_rows, 0)
    scaled = source_scaling.astype(jnp.bfloat16)
    target_scaling = target_mass
    for iteration in range(ITERS):
        column_sums = lax.psum(jnp.dot(scaled, kernel, preferred_element_type=jnp.float32), "row")
        target_scaling = target_mass / column_sums
        if iteration + 1 < ITERS:
            update_right_side = target_scaling.astype(jnp.bfloat16)
            row_sums = lax.psum(row_pass(update_right_side), "col")
            scaled = (source_mass / row_sums).astype(jnp.bfloat16)
    membership = labels[:, None] == jnp.arange(SETS, dtype=jnp.int32)[None, :]
    probes = jnp.where(
        membership, target_scaling.astype(jnp.bfloat16)[:, None], jnp.zeros((), jnp.bfloat16)
    )
    all_sums = lax.psum(row_pass(probes), "col")
    own_sums = lax.dynamic_slice_in_dim(all_sums, own_first, share_rows, 0)
    totals = jnp.sum(own_sums, 1)
    fates = own_sums / totals[:, None]
    source_potential = entropy_weight * jnp.log(own_mass / totals)
    target_potential = entropy_weight * jnp.log(target_scaling)
    return (fates, source_potential, target_potential)


def solution(mesh):
    placed = (P("row", None), P("col", None), P("row"), P("col"), P("row"), P("col"))
    return jax.shard_map(
        on_device,
        mesh=mesh,
        in_specs=placed,
        out_specs=(P(("row", "col"), None), P(("row", "col")), P("col")),
        check_vma=False,
    )
```

profile of v0, /device:TPU:2, one launch (start us, length us, event | category | flops | bytes accessed | tf_op | source)
XLA Modules:
  0.0 551.6 jit_solution(15440935241534829660)
XLA Ops:
  7.2 2.2 convert_reduce_fusion
  9.5 12.3 %all-reduce.1 = (f32[]{:T(128)}, f32[64]{0:T(128)S(1)}) all-reduce(f32[]{:T(128)} %get-tuple-element.75, f32[64]{0:T(128)S(1)} %get-tuple-element.76), channel_id=1, replica_groups=mesh['row'=8,'col'=32] {'row'}, use_global_device_ids=true, to_apply=%region_3.0 | all-reduce | flops 65 | bytes 520 | tf_op jit(solution)/shard_map/psum | solution.py:29
  22.4 78.6 %all-reduce = (f32[]{:T(128)}, f32[64]{0:T(128)S(1)}) all-reduce(f32[]{:T(128)} %get-tuple-element.50, f32[64]{0:T(128)S(1)} %get-tuple-element.49), channel_id=1, replica_groups=mesh['row'=8,'col'=32] {'col'}, use_global_device_ids=true, to_apply=%region_5.0 | all-reduce | flops 65 | bytes 520 | tf_op jit(solution)/shard_map/psum | solution.py:30
  101.6 0.6 multiply_reduce_fusion
  102.9 52.0 %while.10 = (s32[]{:T(128)}, bf16[8,512,4096]{2,1,0:T(8,128)(2,1)}, s32[8]{0:T(128)S(1)}, f32[4096]{0:T(1024)S(1)}, f32[4096]{0:T(1024)S(1)}, /*index=5*/bf16[40...) while((s32[]{:T(128)}, bf16[8,512,4096]{2,1,0:T(8,128)(2,1)}, ...), condition=%wide.region_12.13_spmd, body=%wide.region_11.12_spmd.sunk | while | flops 281018368 | bytes 4807863 | solution.py:54
  104.3 5.2 fusion.31
  110.7 5.2 fusion.31
  117.3 5.2 fusion.31
  123.8 5.2 fusion.31
  130.3 5.2 fusion.31
  136.8 5.2 fusion.31
  143.3 5.2 fusion.31
  149.8 5.2 fusion.31
  155.0 12.8 %fusion.15 = f32[1,4096]{1,0:T(1,128)S(1)} fusion(bf16[4096,4096]{1,0:T(8,128)(2,1)} %bitcast.23, bf16[4096,1]{0,1:T(2,128)(2,1)S(1)} %reshape.17), kind=kOutput, calls=%fused_computation.29 | convolution fusion | flops 33554432 | bytes 33579008 | tf_op jit(solution)/shard_map/dot_general | solution.py:67
  167.8 23.6 %psum.60 = f32[4096]{0:T(1024)S(1)} all-reduce(f32[4096]{0:T(1024)S(1)} %bitcast.28), channel_id=1, replica_groups=mesh['row'=8,'col'=32] {'row'}, use_global_device_ids=true, to_apply=%region_13.14 | all-reduce | flops 4096 | bytes 32768 | tf_op jit(solution)/shard_map/psum | solution.py:67
  191.5 15.0 %fusion.16 = f32[1,4096]{1,0:T(1,128)S(1)} fusion(bf16[4096,4096]{1,0:T(8,128)(2,1)} %bitcast.24, bf16[4096,1]{0,1:T(2,128)(2,1)S(1)} %reshape.19), kind=kOutput, calls=%fused_computation.30 | convolution fusion | flops 33554432 | bytes 33579008 | tf_op jit(solution)/shard_map/dot_general | solution.py:59
  206.5 137.7 %psum.61 = f32[4096]{0:T(1024)S(1)} all-reduce(f32[4096]{0:T(1024)S(1)} %bitcast.27), channel_id=1, replica_groups=mesh['row'=8,'col'=32] {'col'}, use_global_device_ids=true, to_apply=%region_14.15 | all-reduce | flops 4096 | bytes 32768 | tf_op jit(solution)/shard_map/psum | solution.py:71
  344.2 12.8 %fusion.17 = f32[1,4096]{1,0:T(1,128)S(1)} fusion(bf16[4096,1]{0,1:T(2,128)(2,1)S(1)} %reshape.21, bf16[4096,4096]{1,0:T(8,128)(2,1)} %bitcast.25), kind=kOutput, calls=%fused_computation.31 | convolution fusion | flops 33554432 | bytes 33579008 | tf_op jit(solution)/shard_map/dot_general | solution.py:67
  357.0 23.7 %psum.62 = f32[4096]{0:T(1024)S(1)} all-reduce(f32[4096]{0:T(1024)S(1)} %bitcast.29), channel_id=1, replica_groups=mesh['row'=8,'col'=32] {'row'}, use_global_device_ids=true, to_apply=%region_15.16 | all-reduce | flops 4096 | bytes 32768 | tf_op jit(solution)/shard_map/psum | solution.py:67
  380.7 0.6 log_multiply_fusion
  381.4 16.6 %fusion.9 = f32[4096,32]{0,1:T(8,128)} fusion(bf16[4096,4096]{1,0:T(8,128)(2,1)} %bitcast.26, s32[4096]{0:T(1024)S(1)} %copy-done.2, bf16[4096]{0:T(1024)(128)(2,1)S(1)} %get-tuple-element.73), kind=kOutput, calls=%fused_computation.15 | convolution fusion | flops 1074003968 | bytes 34103296 | tf_op jit(solution)/shard_map/dot_general | solution.py:59
  398.0 144.0 %all-reduce.4.cloned.1.call-done = f32[4096,32]{0,1:T(8,128)} async-done(((f32[4096,32]{0,1:T(8,128)}), f32[4096,32]{0,1:T(8,128)}) %all-reduce.4.cloned.1.call-update) | async-done | bytes 524304 | tf_op jit(solution)/shard_map/psum | solution.py:77
  542.1 0.7 dynamic-slice_reduce_fusion
  543.4 1.3 dynamic-slice_divide_fusion
  (35 shorter events, 6.0 us)
Async XLA Ops:
  7.2 534.9 %all-reduce.4.cloned.1.call-start = ((), (), s32[]{:S(2)}) async-start(), calls=%async_computation | async-start | bytes 1048576 | tf_op jit(solution)/shard_map/psum | solution.py:77
  102.9 52.0 %copy-start.3 = (f32[4096]{0:T(1024)S(1)}, f32[4096]{0:T(1024)}, u32[]{:S(2)}) copy-start(f32[4096]{0:T(1024)} %param.12) | copy-start | bytes 49156
  155.0 36.5 %copy-start = (f32[4096]{0:T(1024)S(1)}, f32[4096]{0:T(1024)}, u32[]{:S(2)}) copy-start(f32[4096]{0:T(1024)} %param.11) | copy-start | bytes 49156
  155.0 189.2 %copy-start.1 = (f32[4096]{0:T(1024)S(1)}, f32[4096]{0:T(1024)}, u32[]{:S(2)}) copy-start(f32[4096]{0:T(1024)} %param.10) | copy-start | bytes 49156
  191.5 189.9 %copy-start.2 = (s32[4096]{0:T(1024)S(1)}, s32[4096]{0:T(1024)}, u32[]{:S(2)}) copy-start(s32[4096]{0:T(1024)} %param.13) | copy-start | bytes 49156
Sparse Core Ops, SparseCore 0:
  398.2 143.8 all-reduce.3
where the time goes:
time: 552 us
  blocking collectives  276 us (50%)
  waiting for transfers between devices  144 us (26%)
  matrix products  98.7 us (18%)
  between operations  16.1 us (3%)
  other arithmetic  6.15 us (1%)
    psum x1, waiting for transfers between devices, on_device(): all_sums = lax.psum(row_pass(probes), 'col')  144 us
    psum x1, blocking collectives, on_device(): row_sums = lax.psum(row_pass(update_right_side), 'col')  138 us
    psum x1, blocking collectives, on_device(): lax.psum((jnp.sum(target_wide, 0), jnp.sum(target_sq)), 'col')  78.6 us
    psum x2, blocking collectives, on_device(): lax.psum(jnp.dot(scaled, kernel, preferred_element_type=jnp.float32), 'row')  47.3 us
    dot_general x8, matrix products, kernel_rows(): lax.dot_general(source_block, target_pcs, (((1,), (1,)), ((), ())), prefe...  41.5 us
    dot_general x2, matrix products, row_pass(): return jnp.dot(kernel, right_side, preferred_element_type=jnp.float32)  31.6 us
    dot_general x2, matrix products, on_device(): jnp.dot(scaled, kernel, preferred_element_type=jnp.float32)  25.7 us
    psum x1, blocking collectives, on_device(): lax.psum((jnp.sum(source_wide, 0), jnp.sum(source_sq)), 'row')  12.3 us
  transfers between devices with their start and end apart: 1, of which 1 were waited for; matrix products, arithmetic and copies ran while one was open for 0% of the time, Pallas kernels for 0%

commit v1 on v0

--- a/solution.py
+++ b/solution.py
@@ -68,7 +68,7 @@
         target_scaling = target_mass / column_sums
         if iteration + 1 < ITERS:
             update_right_side = target_scaling.astype(jnp.bfloat16)
-            row_sums = lax.psum(row_pass(update_right_side), "col")
+            row_sums = jnp.sum(lax.all_gather(row_pass(update_right_side), "col"), axis=0)
             scaled = (source_mass / row_sums).astype(jnp.bfloat16)
     membership = labels[:, None] == jnp.arange(SETS, dtype=jnp.int32)[None, :]
     probes = jnp.where(

time: 552 us -> 464 us (0.84)
  blocking collectives: 276 us -> 185 us
    psum x1 -> x0, blocking collectives: 138 us -> none  [on_device(): row_sums = lax.psum(row_pass(update_right_side), 'col')]
    all_gather x0 -> x1, blocking collectives: none -> 46.3 us  [on_device(): lax.all_gather(row_pass(update_right_side), 'col')]
where the time goes in v1:
time: 464 us; the launch traced here: 463 us
  blocking collectives  185 us (40%)
  waiting for transfers between devices  147 us (32%)
  matrix products  98.7 us (21%)
  between operations  16.1 us (3%)
  other arithmetic  6.2 us (1%)
  local copies, waits for them, and re-layouts  5.44 us (1%)
  loops' own time  5.28 us (1%)
    psum x1, waiting for transfers between devices, on_device(): all_sums = lax.psum(row_pass(probes), 'col')  147 us
    psum x1, blocking collectives, on_device(): lax.psum((jnp.sum(target_wide, 0), jnp.sum(target_sq)), 'col')  78.6 us
    psum x2, blocking collectives, on_device(): lax.psum(jnp.dot(scaled, kernel, preferred_element_type=jnp.float32), 'row')  47.4 us
    all_gather x1, blocking collectives, on_device(): lax.all_gather(row_pass(update_right_side), 'col')  46.3 us
    dot_general x8, matrix products, kernel_rows(): lax.dot_general(source_block, target_pcs, (((1,), (1,)), ((), ())), prefe...  41.5 us
    dot_general x2, matrix products, row_pass(): return jnp.dot(kernel, right_side, preferred_element_type=jnp.float32)  31.6 us
    dot_general x2, matrix products, on_device(): jnp.dot(scaled, kernel, preferred_element_type=jnp.float32)  25.7 us
    psum x1, blocking collectives, on_device(): lax.psum((jnp.sum(source_wide, 0), jnp.sum(source_sq)), 'row')  12.3 us
  transfers between devices with their start and end apart: 1, of which 1 were waited for; matrix products, arithmetic and copies ran while one was open for 0% of the time, Pallas kernels for 0%

profile of v1, /device:TPU:2, one launch (start us, length us, event | category | flops | bytes accessed | tf_op | source)
XLA Modules:
  0.0 463.0 jit_solution(607848139816923332)
XLA Ops:
  7.2 2.2 convert_reduce_fusion
  9.5 12.3 %all-reduce.1 = (f32[]{:T(128)}, f32[64]{0:T(128)S(1)}) all-reduce(f32[]{:T(128)} %get-tuple-element.75, f32[64]{0:T(128)S(1)} %get-tuple-element.76), channel_id=1, replica_groups=mesh['row'=8,'col'=32] {'row'}, use_global_device_ids=true, to_apply=%region_3.0 | all-reduce | flops 65 | bytes 520 | tf_op jit(solution)/shard_map/psum | solution.py:29
  22.4 78.6 %all-reduce = (f32[]{:T(128)}, f32[64]{0:T(128)S(1)}) all-reduce(f32[]{:T(128)} %get-tuple-element.50, f32[64]{0:T(128)S(1)} %get-tuple-element.49), channel_id=1, replica_groups=mesh['row'=8,'col'=32] {'col'}, use_global_device_ids=true, to_apply=%region_5.0 | all-reduce | flops 65 | bytes 520 | tf_op jit(solution)/shard_map/psum | solution.py:30
  101.6 0.6 multiply_reduce_fusion
  102.9 52.0 %while.10 = (s32[]{:T(128)}, bf16[8,512,4096]{2,1,0:T(8,128)(2,1)}, s32[8]{0:T(128)S(1)}, f32[4096]{0:T(1024)S(1)}, f32[4096]{0:T(1024)S(1)}, /*index=5*/bf16[40...) while((s32[]{:T(128)}, bf16[8,512,4096]{2,1,0:T(8,128)(2,1)}, ...), condition=%wide.region_12.13_spmd, body=%wide.region_11.12_spmd.sunk | while | flops 281018368 | bytes 4807863 | solution.py:54
  104.3 5.2 %fusion.31 = bf16[8,512,4096]{2,1,0:T(8,128)(2,1)} fusion(bf16[8,512,4096]{2,1,0:T(8,128)(2,1)} %get-tuple-element.139, s32[]{:T(128)} %get-tuple-element.138, bf16[4096,64]{0,1:T(8,128)(2,1)} %get-tuple-element.156, f32[]{:T(128)} %get-tuple-element.157, f32[4096]{0:T(1024)S(1)} %get-tuple-element.154, f32[512]{0:T(512)S(1)} %dynamic_slice.30, ...), kind=kOutput, calls=%fused_computation.2.clone.1 | convolution fusion | flops 281018368 | bytes 4803588 | tf_op jit(solution)/shard_map/while/body/eval_jaxpr/dot_general | solution.py:15
  110.7 5.2 %fusion.31 = bf16[8,512,4096]{2,1,0:T(8,128)(2,1)} fusion(bf16[8,512,4096]{2,1,0:T(8,128)(2,1)} %get-tuple-element.139, s32[]{:T(128)} %get-tuple-element.138, bf16[4096,64]{0,1:T(8,128)(2,1)} %get-tuple-element.156, f32[]{:T(128)} %get-tuple-element.157, f32[4096]{0:T(1024)S(1)} %get-tuple-element.154, f32[512]{0:T(512)S(1)} %dynamic_slice.30, ...), kind=kOutput, calls=%fused_computation.2.clone.1 | convolution fusion | flops 281018368 | bytes 4803588 | tf_op jit(solution)/shard_map/while/body/eval_jaxpr/dot_general | solution.py:15
  117.3 5.2 %fusion.31 = bf16[8,512,4096]{2,1,0:T(8,128)(2,1)} fusion(bf16[8,512,4096]{2,1,0:T(8,128)(2,1)} %get-tuple-element.139, s32[]{:T(128)} %get-tuple-element.138, bf16[4096,64]{0,1:T(8,128)(2,1)} %get-tuple-element.156, f32[]{:T(128)} %get-tuple-element.157, f32[4096]{0:T(1024)S(1)} %get-tuple-element.154, f32[512]{0:T(512)S(1)} %dynamic_slice.30, ...), kind=kOutput, calls=%fused_computation.2.clone.1 | convolution fusion | flops 281018368 | bytes 4803588 | tf_op jit(solution)/shard_map/while/body/eval_jaxpr/dot_general | solution.py:15
  123.8 5.2 %fusion.31 = bf16[8,512,4096]{2,1,0:T(8,128)(2,1)} fusion(bf16[8,512,4096]{2,1,0:T(8,128)(2,1)} %get-tuple-element.139, s32[]{:T(128)} %get-tuple-element.138, bf16[4096,64]{0,1:T(8,128)(2,1)} %get-tuple-element.156, f32[]{:T(128)} %get-tuple-element.157, f32[4096]{0:T(1024)S(1)} %get-tuple-element.154, f32[512]{0:T(512)S(1)} %dynamic_slice.30, ...), kind=kOutput, calls=%fused_computation.2.clone.1 | convolution fusion | flops 281018368 | bytes 4803588 | tf_op jit(solution)/shard_map/while/body/eval_jaxpr/dot_general | solution.py:15
  130.3 5.2 %fusion.31 = bf16[8,512,4096]{2,1,0:T(8,128)(2,1)} fusion(bf16[8,512,4096]{2,1,0:T(8,128)(2,1)} %get-tuple-element.139, s32[]{:T(128)} %get-tuple-element.138, bf16[4096,64]{0,1:T(8,128)(2,1)} %get-tuple-element.156, f32[]{:T(128)} %get-tuple-element.157, f32[4096]{0:T(1024)S(1)} %get-tuple-element.154, f32[512]{0:T(512)S(1)} %dynamic_slice.30, ...), kind=kOutput, calls=%fused_computation.2.clone.1 | convolution fusion | flops 281018368 | bytes 4803588 | tf_op jit(solution)/shard_map/while/body/eval_jaxpr/dot_general | solution.py:15
  136.8 5.2 %fusion.31 = bf16[8,512,4096]{2,1,0:T(8,128)(2,1)} fusion(bf16[8,512,4096]{2,1,0:T(8,128)(2,1)} %get-tuple-element.139, s32[]{:T(128)} %get-tuple-element.138, bf16[4096,64]{0,1:T(8,128)(2,1)} %get-tuple-element.156, f32[]{:T(128)} %get-tuple-element.157, f32[4096]{0:T(1024)S(1)} %get-tuple-element.154, f32[512]{0:T(512)S(1)} %dynamic_slice.30, ...), kind=kOutput, calls=%fused_computation.2.clone.1 | convolution fusion | flops 281018368 | bytes 4803588 | tf_op jit(solution)/shard_map/while/body/eval_jaxpr/dot_general | solution.py:15
  143.3 5.2 %fusion.31 = bf16[8,512,4096]{2,1,0:T(8,128)(2,1)} fusion(bf16[8,512,4096]{2,1,0:T(8,128)(2,1)} %get-tuple-element.139, s32[]{:T(128)} %get-tuple-element.138, bf16[4096,64]{0,1:T(8,128)(2,1)} %get-tuple-element.156, f32[]{:T(128)} %get-tuple-element.157, f32[4096]{0:T(1024)S(1)} %get-tuple-element.154, f32[512]{0:T(512)S(1)} %dynamic_slice.30, ...), kind=kOutput, calls=%fused_computation.2.clone.1 | convolution fusion | flops 281018368 | bytes 4803588 | tf_op jit(solution)/shard_map/while/body/eval_jaxpr/dot_general | solution.py:15
  149.8 5.2 %fusion.31 = bf16[8,512,4096]{2,1,0:T(8,128)(2,1)} fusion(bf16[8,512,4096]{2,1,0:T(8,128)(2,1)} %get-tuple-element.139, s32[]{:T(128)} %get-tuple-element.138, bf16[4096,64]{0,1:T(8,128)(2,1)} %get-tuple-element.156, f32[]{:T(128)} %get-tuple-element.157, f32[4096]{0:T(1024)S(1)} %get-tuple-element.154, f32[512]{0:T(512)S(1)} %dynamic_slice.30, ...), kind=kOutput, calls=%fused_computation.2.clone.1 | convolution fusion | flops 281018368 | bytes 4803588 | tf_op jit(solution)/shard_map/while/body/eval_jaxpr/dot_general | solution.py:15
  155.0 12.8 %fusion.15 = f32[1,4096]{1,0:T(1,128)S(1)} fusion(bf16[4096,4096]{1,0:T(8,128)(2,1)} %bitcast.23, bf16[4096,1]{0,1:T(2,128)(2,1)S(1)} %reshape.18), kind=kOutput, calls=%fused_computation.29 | convolution fusion | flops 33554432 | bytes 33579008 | tf_op jit(solution)/shard_map/dot_general | solution.py:67
  167.8 23.6 %psum.53 = f32[4096]{0:T(1024)S(1)} all-reduce(f32[4096]{0:T(1024)S(1)} %bitcast.28), channel_id=1, replica_groups=mesh['row'=8,'col'=32] {'row'}, use_global_device_ids=true, to_apply=%region_13.14 | all-reduce | flops 4096 | bytes 32768 | tf_op jit(solution)/shard_map/psum | solution.py:67
  191.5 15.0 %fusion.16 = f32[1,4096]{1,0:T(1,128)S(1)} fusion(bf16[4096,4096]{1,0:T(8,128)(2,1)} %bitcast.24, bf16[4096,1]{0,1:T(2,128)(2,1)S(1)} %reshape.20), kind=kOutput, calls=%fused_computation.30 | convolution fusion | flops 33554432 | bytes 33579008 | tf_op jit(solution)/shard_map/dot_general | solution.py:59
  206.5 46.3 %all-gather = f32[131072]{0:T(1024)S(1)} all-gather(f32[4096]{0:T(1024)S(1)} %bitcast.27), channel_id=2, replica_groups=mesh['row'=8,'col'=32] {'col'}, dimensions={0}, use_global_device_ids=true | all-gather | bytes 540672 | tf_op jit(solution)/shard_map/all_gather | solution.py:71
  253.0 12.8 %fusion.17 = f32[1,4096]{1,0:T(1,128)S(1)} fusion(bf16[4096,1]{0,1:T(2,128)(2,1)S(1)} %reshape.22, bf16[4096,4096]{1,0:T(8,128)(2,1)} %bitcast.25), kind=kOutput, calls=%fused_computation.31 | convolution fusion | flops 33554432 | bytes 33579008 | tf_op jit(solution)/shard_map/dot_general | solution.py:67
  265.8 23.8 %psum.54 = f32[4096]{0:T(1024)S(1)} all-reduce(f32[4096]{0:T(1024)S(1)} %bitcast.29), channel_id=1, replica_groups=mesh['row'=8,'col'=32] {'row'}, use_global_device_ids=true, to_apply=%region_15.16 | all-reduce | flops 4096 | bytes 32768 | tf_op jit(solution)/shard_map/psum | solution.py:67
  289.6 0.6 log_multiply_fusion
  290.2 16.6 %fusion.9 = f32[4096,32]{0,1:T(8,128)} fusion(bf16[4096,4096]{1,0:T(8,128)(2,1)} %bitcast.26, s32[4096]{0:T(1024)S(1)} %copy-done.2, bf16[4096]{0:T(1024)(128)(2,1)S(1)} %get-tuple-element.73), kind=kOutput, calls=%fused_computation.15 | convolution fusion | flops 1074003968 | bytes 34103296 | tf_op jit(solution)/shard_map/dot_general | solution.py:59
  306.9 146.6 %all-reduce.4.cloned.1.call-done = f32[4096,32]{0,1:T(8,128)} async-done(((f32[4096,32]{0,1:T(8,128)}), f32[4096,32]{0,1:T(8,128)}) %all-reduce.4.cloned.1.call-update) | async-done | bytes 524304 | tf_op jit(solution)/shard_map/psum | solution.py:77
  453.5 0.7 dynamic-slice_reduce_fusion
  454.8 1.3 dynamic-slice_divide_fusion
  (37 shorter events, 6.2 us)
Async XLA Ops:
  7.2 446.3 %all-reduce.4.cloned.1.call-start = ((), (), s32[]{:S(2)}) async-start(), calls=%async_computation | async-start | bytes 1048576 | tf_op jit(solution)/shard_map/psum | solution.py:77
  102.9 52.0 %copy-start.3 = (f32[4096]{0:T(1024)S(1)}, f32[4096]{0:T(1024)}, u32[]{:S(2)}) copy-start(f32[4096]{0:T(1024)} %param.12) | copy-start | bytes 49156
  155.0 36.5 %copy-start = (f32[4096]{0:T(1024)S(1)}, f32[4096]{0:T(1024)}, u32[]{:S(2)}) copy-start(f32[4096]{0:T(1024)} %param.11) | copy-start | bytes 49156
  155.0 98.0 %copy-start.1 = (f32[4096]{0:T(1024)S(1)}, f32[4096]{0:T(1024)}, u32[]{:S(2)}) copy-start(f32[4096]{0:T(1024)} %param.10) | copy-start | bytes 49156
  191.5 98.8 %copy-start.2 = (s32[4096]{0:T(1024)S(1)}, s32[4096]{0:T(1024)}, u32[]{:S(2)}) copy-start(s32[4096]{0:T(1024)} %param.13) | copy-start | bytes 49156
Sparse Core Ops, SparseCore 0:
  307.0 146.4 all-reduce.3
